TPU v7x, 32 devices: a whole 2x2x4 slice. The times are simulated.
32 devices in a mesh: groups: 2 (over x), vid: 8 (over z, y), tok: 2 (over core).
Axes of the slice: x: 2, y: 2, z: 4, core: 2. Of those that a mesh axis runs over, the one named last changes fastest.
Arguments:
- captions: bfloat16 [16, 128, 32, 128], P(('groups', 'vid')), parts along dimension 0, may hold values from -8 to 8
- caption_lengths: int32 [16, 128], P(('groups', 'vid')), parts along dimension 0, may hold values from 1 to 32
- video_bank: bfloat16 [192, 256, 128], P(('groups', 'vid'), 'tok'), parts along dimension 0, may hold values from -1.5 to 1.5
- owner_order: int32 [6], P('groups'), parts along dimension 0, may hold values from 0 to 7, as said below
Outputs:
- scores: float32 [192, 384], P(('groups', 'vid')), parts along dimension 0
There are 2 independent parts, one for each index of `groups`. A program takes and returns all parts, laid end to end along the dimension named above; each array names one. Nothing has to cross between parts.
Inputs may be any that keep to these rules, and one draw needn't show every extreme that they name: `caption_lengths`: token slot j of a caption is real when j is less than its count. `owner_order`: 3 different block indices.
All inputs are finite; a program needn't handle non-finite values.
Results may differ from a plain program's by a relative error of at most 0.0003.
Values may be sent and summed in bfloat16 or wider, within the bound.
No kernel may reach another device: no remote copies, remote signals or barrier semaphores. Data moves between devices by JAX's collectives and lax.ppermute only.
A program may use at most 64 MiB of HBM per device.

v0:
```python
import jax
import jax.numpy as jnp
from jax import lax
from jax.sharding import PartitionSpec as P

ROUNDS = 3
sharpness_factor = 5.0


def spread(value, axis, source):
    kept = jnp.where(lax.axis_index(axis) == source, value, 0).astype(value.dtype)
    return lax.psum(kept, axis)


def mask_weights(counts, slot_count):
    slots = jnp.arange(slot_count, dtype=jnp.int32)
    lengths_float = counts.astype(jnp.float32)
    return (slots[None, :] < counts[:, None]).astype(jnp.float32) / lengths_float[:, None]


def per_device(captions, caption_lengths, video_bank, owner_order):
    results = []
    bank_whole = lax.all_gather(video_bank, "tok", axis=1, tiled=True)
    share_rows = captions.shape[1] // lax.axis_size("tok")
    start_row = lax.axis_index("tok") * share_rows
    for round_index in range(ROUNDS):
        owner_now = owner_order[round_index]
        my_share = lax.dynamic_slice_in_dim(captions[0], start_row, share_rows, 0)
        my_counts = lax.dynamic_slice_in_dim(caption_lengths[0], start_row, share_rows, 0)
        share_rows_now, share_counts = (
            spread(my_share, "vid", owner_now),
            spread(my_counts, "vid", owner_now),
        )
        slot_count = share_rows_now.shape[1]
        query_rows = share_rows_now.reshape(share_rows * slot_count, share_rows_now.shape[2])

        def whole_video(footage_key_matrix):
            raw_similarity = (
                lax.dot_general(
                    query_rows,
                    footage_key_matrix,
                    (((1,), (1,)), ((), ())),
                    preferred_element_type=jnp.float32,
                )
                * sharpness_factor
            )
            row_peak = jnp.max(raw_similarity, axis=1)
            row_accumulated = jnp.sum(jnp.exp(raw_similarity - row_peak[:, None]), axis=1)
            return (row_peak + jnp.log(row_accumulated)) / sharpness_factor

        smoothed_scores = lax.map(whole_video, bank_whole).reshape(
            video_bank.shape[0], share_rows, slot_count
        )
        weights = mask_weights(share_counts, slot_count)
        results.append(
            jnp.einsum("vcj,cj->vc", smoothed_scores, weights, precision=lax.Precision.HIGHEST)
        )
    stacked = jnp.stack(results, axis=1)
    gathered = lax.all_gather(stacked, "tok", axis=2, tiled=True)
    return gathered.reshape(video_bank.shape[0], ROUNDS * captions.shape[1])


def solution(mesh):
    return jax.shard_map(
        per_device,
        mesh=mesh,
        in_specs=(
            P(("groups", "vid"), None, None, None),
            P(("groups", "vid"), None),
            P(("groups", "vid"), "tok", None),
            P("groups"),
        ),
        out_specs=P(("groups", "vid"), None),
        check_vma=False,
    )
```

profile of v0, /device:TPU:0, one launch (start us, length us, event | category | flops | bytes accessed | tf_op | source)
XLA Modules:
  0.0 167.1 jit_solution(8382262049726424937)
XLA Ops:
  6.5 1.4 fusion.21
  9.9 2.3 %broadcast_select_fusion.2 = (bf16[1,64,32,128]{3,2,1,0:T(8,128)(2,1)}, bf16[1,64,32,128]{3,2,1,0:T(8,128)(2,1)}, bf16[1,64,32,128]{3,2,1,0:T(8,128)(2,1)}) fusion(pred[]{:T(512)S(6)} %eq.12, bf16[1,128,32,128]{3,2,1,0:T(8,128)(2,1)} %param.10, s32[]{:T(128)S(6)} %select_n.67, pred[]{:T(512)S(6)} %eq.13, pred[]{:T(512)S(6)} %eq.14), kind=kLoop, calls=%fused_computation.26 | loop fusion | flops 786432 | bytes 2097159 | tf_op jit(solution)/shard_map/jit(_where)/select_n | solution.py:11
  12.3 13.5 %all-reduce = (s32[64]{0:T(128)S(1)}, s32[64]{0:T(128)S(1)}, s32[64]{0:T(128)S(1)}) all-reduce(s32[64]{0:T(128)S(1)} %get-tuple-element.115, s32[64]{0:T(128)S(1)} %get-tuple-element.114, s32[64]{0:T(128)S(1)} %get-tuple-element.113), channel_id=1, replica_groups=mesh['groups'=2,'vid'=8,'tok'=2] {'vid'}, use_global_device_ids=true, to_apply=%region_12.13 | all-reduce | flops 192 | bytes 1536 | tf_op jit(solution)/shard_map/psum | solution.py:12
  25.8 2.4 %all_gather.6 = bf16[12,256,128]{2,1,0:T(8,128)(2,1)S(1)} all-gather(bf16[12,128,128]{2,1,0:T(8,128)(2,1)S(1)} %copy-done.2), channel_id=1, replica_groups=mesh['groups'=2,'vid'=8,'tok'=2] {'tok'}, dimensions={1}, use_global_device_ids=true | all-gather | bytes 1179648 | tf_op jit(solution)/shard_map/all_gather | solution.py:23
  28.4 76.2 %all-reduce.4.cloned.1.call-done = (bf16[2048,128]{1,0:T(8,128)(2,1)}, bf16[2048,128]{1,0:T(8,128)(2,1)}, bf16[2048,128]{1,0:T(8,128)(2,1)}) async-done(((bf16[2048,128]{1,0:T(8,128)(2,1)}, bf16[2048,128]{1,0:T(8,128)(2,1)}, bf16[2048,128]{1,0:T(8,128)(2,1)}), (bf16[2048,128]{1,0:T(8,128)(2,1)}, bf16[2048,128]{1,0:T(8,128)(2,1)}, bf16[2048,128]{1,0:T(8,128)(2,1)})) %all-reduce.4.cloned.1.call-update) | async-done | bytes 1572880 | tf_op jit(solution)/shard_map/psum | solution.py:12
  104.6 24.6 %while.30 = (s32[]{:T(128)}, f32[12,2048]{1,0:T(8,128)S(1)}, bf16[12,256,128]{2,1,0:T(8,128)(2,1)S(1)}, bf16[2048,128]{1,0:T(8,128)(2,1)}, s32[]{:T(128)}, /*index=5*/s32[]{:T(128)}) while((s32[]{:T(128)}, f32[12,2048]{1,0:T(8,128)S(1)}, bf16[12,256,128]{2,1,0:T(8,128)(2,1)S(1)}, bf16[2048,128]{1,0:T(8,128)(2,1)}, s32[]{:T(128)}, ...), condition=%wide.region_5.6_spmd, body=%wide.region_2.5_spmd.sunk | while | flops 136314880 | bytes 4849741 | solution.py:51
  104.6 1.5 fusion.35
  106.7 1.5 fusion.35
  108.8 1.5 fusion.35
  110.8 1.5 fusion.35
  112.9 1.5 fusion.35
  114.9 1.5 fusion.35
  117.0 1.5 fusion.35
  119.0 1.5 fusion.35
  121.1 1.5 fusion.35
  123.1 1.5 fusion.35
  125.2 1.5 fusion.35
  127.2 1.5 fusion.35
  129.4 1.1 fusion.13
  130.6 12.0 %while.31 = (s32[]{:T(128)}, f32[12,2048]{1,0:T(8,128)S(1)}, bf16[12,256,128]{2,1,0:T(8,128)(2,1)S(1)}, bf16[2048,128]{1,0:T(8,128)(2,1)S(1)}, s32[]{:T(128)}, /*index=5*/s32[]{:T(128)}) while((s32[]{:T(128)}, f32[12,2048]{1,0:T(8,128)S(1)}, bf16[12,256,128]{2,1,0:T(8,128)(2,1)S(1)}, bf16[2048,128]{1,0:T(8,128)(2,1)S(1)}, s32[]{:T(128)}, ...), condition=%wide.region_11.12_spmd, body=%wide.region_8.11_spmd.sunk | while | flops 136314880 | bytes 4849741 | solution.py:51
  142.8 1.1 fusion.11
  144.0 12.0 %while.32 = (s32[]{:T(128)}, f32[12,2048]{1,0:T(8,128)S(1)}, bf16[12,256,128]{2,1,0:T(8,128)(2,1)S(1)}, bf16[2048,128]{1,0:T(8,128)(2,1)S(1)}, s32[]{:T(128)}, /*index=5*/s32[]{:T(128)}) while((s32[]{:T(128)}, f32[12,2048]{1,0:T(8,128)S(1)}, bf16[12,256,128]{2,1,0:T(8,128)(2,1)S(1)}, bf16[2048,128]{1,0:T(8,128)(2,1)S(1)}, s32[]{:T(128)}, ...), condition=%wide.region_17.18_spmd, body=%wide.region_14.17_spmd.sunk | while | flops 136314880 | bytes 4849741 | solution.py:51
  156.2 1.1 fusion.9
  157.6 2.0 %all_gather.7 = f32[12,3,128]{0,1,2:T(4,128)S(1)} all-gather(f32[12,3,64]{0,1,2:T(4,128)S(1)} %copy.6), channel_id=1, replica_groups=mesh['groups'=2,'vid'=8,'tok'=2] {'tok'}, dimensions={2}, use_global_device_ids=true | all-gather | bytes 27648 | tf_op jit(solution)/shard_map/all_gather | solution.py:59
  (162 shorter events, 31.4 us)
Async XLA Ops:
  6.5 5.7 %copy-start.3 = (s32[1,128]{1,0:T(1,128)S(1)}, s32[1,128]{1,0:T(1,128)}, u32[]{:S(2)}) copy-start(s32[1,128]{1,0:T(1,128)} %param.11) | copy-start | bytes 1540
  6.5 19.3 %copy-start.2 = (bf16[12,128,128]{2,1,0:T(8,128)(2,1)S(1)}, bf16[12,128,128]{2,1,0:T(8,128)(2,1)}, u32[]{:S(2)}) copy-start(bf16[12,128,128]{2,1,0:T(8,128)(2,1)} %param.12) | copy-start | bytes 1179652
  6.5 98.1 %all-reduce.4.cloned.1.call-start = ((), (), s32[]{:S(2)}) async-start(), calls=%async_computation | async-start | bytes 3145728 | tf_op jit(solution)/shard_map/psum | solution.py:12
  104.6 26.0 %copy-start.1 = (bf16[2048,128]{1,0:T(8,128)(2,1)S(1)}, bf16[2048,128]{1,0:T(8,128)(2,1)}, u32[]{:S(2)}) copy-start(bf16[2048,128]{1,0:T(8,128)(2,1)} %get-tuple-element.229) | copy-start | bytes 1572868
  130.6 13.4 %copy-start = (bf16[2048,128]{1,0:T(8,128)(2,1)S(1)}, bf16[2048,128]{1,0:T(8,128)(2,1)}, u32[]{:S(2)}) copy-start(bf16[2048,128]{1,0:T(8,128)(2,1)} %get-tuple-element.211) | copy-start | bytes 1572868
Sparse Core Ops, SparseCore 0:
  12.3 92.2 all-reduce.3
where the time goes:
time: 168 us; the launch traced here: 167 us
  waiting for transfers between devices  76.2 us (45%)
  matrix products  31.9 us (19%)
  blocking collectives  17.9 us (11%)
  between operations  15.4 us (9%)
  other arithmetic  14.1 us (8%)
  local copies, waits for them, and re-layouts  10.4 us (6%)
    psum x1, waiting for transfers between devices, spread(): return lax.psum(kept, axis)  76.2 us
    dot_general x36, matrix products, whole_video(): lax.dot_general(query_rows, footage_key_matrix, (((1,), (1,)), ((), ())),...  28.5 us
    psum x1, blocking collectives, spread(): return lax.psum(kept, axis)  13.5 us
    reduce_sum x36, other arithmetic, whole_video(): jnp.sum(jnp.exp(raw_similarity - row_peak[:, None]), axis=1)  11.1 us
    dynamic_update_slice x36, local copies, waits for them, and re-layouts, per_device(): lax.map(whole_video, bank_whole)  7.37 us
  transfers between devices with their start and end apart: 1, of which 1 were waited for; matrix products, arithmetic and copies ran while one was open for 0% of the time, Pallas kernels for 0%

commit v1 on v0

--- a/solution.py
+++ b/solution.py
@@ -7,9 +7,15 @@
 sharpness_factor = 5.0
 
 
+def gather_and_add(x, name):
+    parts = lax.all_gather(x, name, axis=0, tiled=False)
+    acc = parts.sum(axis=0)
+    return acc
+
+
 def spread(value, axis, source):
     kept = jnp.where(lax.axis_index(axis) == source, value, 0).astype(value.dtype)
-    return lax.psum(kept, axis)
+    return gather_and_add(kept, axis)
 
 
 def mask_weights(counts, slot_count):

time: 168 us -> 261 us (1.55)
  waiting for transfers between devices: 76.2 us -> 129 us
  blocking collectives: 17.9 us -> 62.5 us
  matrix products: 31.9 us -> 19.3 us
  other arithmetic: 14.1 us -> 23.4 us
    all_gather x0 -> x3, waiting for transfers between devices: none -> 127 us  [gather_and_add(): parts = lax.all_gather(x, name, axis=0, tiled=False)]
    psum x1 -> x0, waiting for transfers between devices: 76.2 us -> none  [spread(): return lax.psum(kept, axis)]
    all_gather x0 -> x3, blocking collectives: none -> 58.1 us  [gather_and_add(): parts = lax.all_gather(x, name, axis=0, tiled=False)]
    psum x1 -> x0, blocking collectives: 13.5 us -> none  [spread(): return lax.psum(kept, axis)]
    dot_general x36, matrix products: 28.5 us -> 15.9 us  [whole_video(): lax.dot_general(query_rows, footage_key_matrix, (((1,), (1,)), ((), ())),...]
    reduce_sum x0 -> x6, other arithmetic: none -> 9.25 us  [gather_and_add(): acc = parts.sum(axis=0)]
  transfers between devices with their start and end apart: 1 -> 3, of which waited for: 1 -> 3; matrix products, arithmetic and copies ran while one was open for 0% -> 12% of each run, Pallas kernels for 0% -> 0%
where the time goes in v1:
time: 261 us
  waiting for transfers between devices  129 us (49%)
  blocking collectives  62.5 us (24%)
  other arithmetic  23.4 us (9%)
  matrix products  19.3 us (7%)
  between operations  15.1 us (6%)
  local copies, waits for them, and re-layouts  10.4 us (4%)
    all_gather x3, waiting for transfers between devices, gather_and_add(): parts = lax.all_gather(x, name, axis=0, tiled=False)  127 us
    all_gather x3, blocking collectives, gather_and_add(): parts = lax.all_gather(x, name, axis=0, tiled=False)  58.1 us
    dot_general x36, matrix products, whole_video(): lax.dot_general(query_rows, footage_key_matrix, (((1,), (1,)), ((), ())),...  15.9 us
    reduce_sum x36, other arithmetic, whole_video(): jnp.sum(jnp.exp(raw_similarity - row_peak[:, None]), axis=1)  11.1 us
    reduce_sum x6, other arithmetic, gather_and_add(): acc = parts.sum(axis=0)  9.25 us
    dynamic_update_slice x36, local copies, waits for them, and re-layouts, per_device(): lax.map(whole_video, bank_whole)  7.37 us
  transfers between devices with their start and end apart: 3, of which 3 were waited for; matrix products, arithmetic and copies ran while one was open for 12% of the time, Pallas kernels for 0%

profile of v1, /device:TPU:0, one launch (start us, length us, event | category | flops | bytes accessed | tf_op | source)
XLA Modules:
  0.0 260.8 jit_solution(16076607981141500725)
XLA Ops:
  6.5 1.4 fusion.21
  9.9 2.3 broadcast_select_fusion.2
  12.2 0.7 all-gather.9.cloned.1.call-update
  13.0 0.7 all-gather.11.cloned.1.call-update
  13.8 22.7 %all-gather = s32[8,1,64]{2,1,0:T(1,128)S(1)} all-gather(s32[1,1,64]{2,1,0:T(1,128)S(1)} %get-tuple-element.107), channel_id=1, replica_groups=mesh['groups'=2,'vid'=8,'tok'=2] {'vid'}, dimensions={0}, use_global_device_ids=true | all-gather | bytes 2304 | tf_op jit(solution)/shard_map/all_gather | solution.py:11
  36.6 2.4 all_gather.31
  38.9 16.5 %all-gather.1 = s32[8,1,64]{2,1,0:T(1,128)S(1)} all-gather(s32[1,1,64]{2,1,0:T(1,128)S(1)} %get-tuple-element.108), channel_id=1, replica_groups=mesh['groups'=2,'vid'=8,'tok'=2] {'vid'}, dimensions={0}, use_global_device_ids=true | all-gather | bytes 2304 | tf_op jit(solution)/shard_map/all_gather | solution.py:11
  55.6 18.9 %all-gather.2 = s32[8,1,64]{2,1,0:T(1,128)S(1)} all-gather(s32[1,1,64]{2,1,0:T(1,128)S(1)} %get-tuple-element.109), channel_id=1, replica_groups=mesh['groups'=2,'vid'=8,'tok'=2] {'vid'}, dimensions={0}, use_global_device_ids=true | all-gather | bytes 2304 | tf_op jit(solution)/shard_map/all_gather | solution.py:11
  74.6 13.3 %all-gather.7.cloned.1.call-done = bf16[8,64,32,128]{3,2,1,0:T(8,128)(2,1)} async-done(((bf16[1,64,32,128]{3,2,1,0:T(8,128)(2,1)}), bf16[8,64,32,128]{3,2,1,0:T(8,128)(2,1)}) %all-gather.7.cloned.1.call-update) | async-done | bytes 4194320 | tf_op jit(solution)/shard_map/all_gather | solution.py:11
  87.9 3.1 %reduce_sum.91 = bf16[64,32,128]{2,1,0:T(8,128)(2,1)S(1)} reduce(bf16[8,64,32,128]{3,2,1,0:T(8,128)(2,1)} %all-gather.7.cloned.1.call-done, bf16[]{:T(256)} %constant.73.clone.1), dimensions={0}, to_apply=%region_1.2 | reduce | flops 1835008 | bytes 4718594 | tf_op jit(solution)/shard_map/reduce_sum | solution.py:12
  91.0 12.0 %while.30 = (s32[]{:T(128)}, f32[12,2048]{1,0:T(8,128)S(1)}, bf16[12,256,128]{2,1,0:T(8,128)(2,1)S(1)}, bf16[2048,128]{1,0:T(8,128)(2,1)S(1)}, s32[]{:T(128)}, /*index=5*/s32[]{:T(128)}) while((s32[]{:T(128)}, f32[12,2048]{1,0:T(8,128)S(1)}, bf16[12,256,128]{2,1,0:T(8,128)(2,1)S(1)}, bf16[2048,128]{1,0:T(8,128)(2,1)S(1)}, s32[]{:T(128)}, ...), condition=%wide.region_5.6_spmd, body=%wide.region_2.5_spmd.sunk | while | flops 136314880 | bytes 4849741 | solution.py:57
  94.0 0.4 fusion.35
  103.2 1.1 fusion.13
  104.4 57.1 %all-gather.9.cloned.1.call-done = bf16[8,64,32,128]{3,2,1,0:T(8,128)(2,1)} async-done(((bf16[1,64,32,128]{3,2,1,0:T(8,128)(2,1)}), bf16[8,64,32,128]{3,2,1,0:T(8,128)(2,1)}) %all-gather.9.cloned.1.call-update) | async-done | bytes 4194320 | tf_op jit(solution)/shard_map/all_gather | solution.py:11
  161.4 3.1 %reduce_sum.93 = bf16[64,32,128]{2,1,0:T(8,128)(2,1)S(1)} reduce(bf16[8,64,32,128]{3,2,1,0:T(8,128)(2,1)} %all-gather.9.cloned.1.call-done, bf16[]{:T(256)} %constant.73.clone.1), dimensions={0}, to_apply=%region_7.8 | reduce | flops 1835008 | bytes 4718594 | tf_op jit(solution)/shard_map/reduce_sum | solution.py:12
  164.5 12.0 %while.31 = (s32[]{:T(128)}, f32[12,2048]{1,0:T(8,128)S(1)}, bf16[12,256,128]{2,1,0:T(8,128)(2,1)S(1)}, bf16[2048,128]{1,0:T(8,128)(2,1)S(1)}, s32[]{:T(128)}, /*index=5*/s32[]{:T(128)}) while((s32[]{:T(128)}, f32[12,2048]{1,0:T(8,128)S(1)}, bf16[12,256,128]{2,1,0:T(8,128)(2,1)S(1)}, bf16[2048,128]{1,0:T(8,128)(2,1)S(1)}, s32[]{:T(128)}, ...), condition=%wide.region_11.12_spmd, body=%wide.region_8.11_spmd.sunk | while | flops 136314880 | bytes 4849741 | solution.py:57
  167.5 0.4 fusion.37
  176.7 1.1 fusion.11
  177.9 57.1 %all-gather.11.cloned.1.call-done = bf16[8,64,32,128]{3,2,1,0:T(8,128)(2,1)} async-done(((bf16[1,64,32,128]{3,2,1,0:T(8,128)(2,1)}), bf16[8,64,32,128]{3,2,1,0:T(8,128)(2,1)}) %all-gather.11.cloned.1.call-update) | async-done | bytes 4194320 | tf_op jit(solution)/shard_map/all_gather | solution.py:11
  235.0 3.1 %reduce_sum.95 = bf16[64,32,128]{2,1,0:T(8,128)(2,1)S(1)} reduce(bf16[8,64,32,128]{3,2,1,0:T(8,128)(2,1)} %all-gather.11.cloned.1.call-done, bf16[]{:T(256)} %constant.73.clone.1), dimensions={0}, to_apply=%region_13.14 | reduce | flops 1835008 | bytes 4718594 | tf_op jit(solution)/shard_map/reduce_sum | solution.py:12
  238.0 12.0 %while.32 = (s32[]{:T(128)}, f32[12,2048]{1,0:T(8,128)S(1)}, bf16[12,256,128]{2,1,0:T(8,128)(2,1)S(1)}, bf16[2048,128]{1,0:T(8,128)(2,1)S(1)}, s32[]{:T(128)}, /*index=5*/s32[]{:T(128)}) while((s32[]{:T(128)}, f32[12,2048]{1,0:T(8,128)S(1)}, bf16[12,256,128]{2,1,0:T(8,128)(2,1)S(1)}, bf16[2048,128]{1,0:T(8,128)(2,1)S(1)}, s32[]{:T(128)}, ...), condition=%wide.region_17.18_spmd, body=%wide.region_14.17_spmd.sunk | while | flops 136314880 | bytes 4849741 | solution.py:57
  250.2 1.1 fusion.9
  251.5 2.0 all_gather.37
  253.7 0.6 copy.17
  (173 shorter events, 35.4 us)
Async XLA Ops:
  6.5 7.1 %copy-start.1 = (s32[1,128]{1,0:T(1,128)S(1)}, s32[1,128]{1,0:T(1,128)}, u32[]{:S(2)}) copy-start(s32[1,128]{1,0:T(1,128)} %param.11) | copy-start | bytes 1540
  6.5 30.0 %copy-start = (bf16[12,128,128]{2,1,0:T(8,128)(2,1)S(1)}, bf16[12,128,128]{2,1,0:T(8,128)(2,1)}, u32[]{:S(2)}) copy-start(bf16[12,128,128]{2,1,0:T(8,128)(2,1)} %param.12) | copy-start | bytes 1179652
  6.5 81.4 %all-gather.7.cloned.1.call-start = ((), (), s32[]{:S(2)}) async-start(), calls=%async_computation | async-start | bytes 4718592 | tf_op jit(solution)/shard_map/all_gather | solution.py:11
  12.2 149.3 %all-gather.9.cloned.1.call-start = ((), (), s32[]{:S(2)}) async-start(), calls=%async_computation.1 | async-start | bytes 4718592 | tf_op jit(solution)/shard_map/all_gather | solution.py:11
  12.9 222.0 %all-gather.11.cloned.1.call-start = ((), (), s32[]{:S(2)}) async-start(), calls=%async_computation.2 | async-start | bytes 4718592 | tf_op jit(solution)/shard_map/all_gather | solution.py:11
Sparse Core Ops, SparseCore 0:
  12.3 75.6 all-gather.6
  90.1 71.3 all-gather.8
  163.6 71.3 all-gather.10
